TPU v7x, 256 devices: a whole 4x4x8 slice. The times are simulated.
256 devices in a mesh: row: 64 (over y, z, core), col: 4 (over x).
Axes of the slice: x: 4, y: 4, z: 8, core: 2. Of those that a mesh axis runs over, the one named last changes fastest.
Arguments:
- factor: float32 [8192, 8192], P('row', 'col'), may hold values from -0.125 to 0.125
- rhs: float32 [8192, 512], P('row', 'col'), may hold values from -6 to 6
- parent: int32 [7], replicated, may hold values from 4 to 6, as said below
- bounds: int32 [8], replicated, may hold values from 0 to 64, as said below
- slot: int32 [64], replicated, may hold values from 0 to 63, each once
- structure: int32 [7, 64], replicated, may hold values 0 or 1
Outputs:
- solution: float32 [8192, 512], P('row', 'col')
Inputs may be any that keep to these rules, and one draw needn't show every extreme that they name: parent[s] is 4 or 5 for s = 0 to 3, and 6 for s = 4, 5, 6 (the root is its own entry). bounds[0] = 0, bounds[7] = 64, strictly increasing; supernode s holds logical blocks bounds[s] to bounds[s+1] - 1. `slot`: a permutation.
All inputs are finite; a program needn't handle non-finite values.
Results may differ from a plain program's by a relative error of at most 0.0001.
Values sent between devices are 32-bit elements; how exact they have to be, the bound alone decides.
A program may use at most 64 MiB of HBM per device.

v0:
```python
import jax
import jax.numpy as jnp
from jax import lax
from jax.sharding import PartitionSpec as P

B = 128
RB = 1


def block_masks(parent, bounds, slot, structure):
    count = slot.shape[0]
    ar = jnp.arange(count, dtype=jnp.int32)
    logical = jnp.sum(jnp.where(slot[:, None] == ar[None, :], ar[:, None], 0), axis=0)
    node = jnp.sum((logical[:, None] >= bounds[None, 1:7]).astype(jnp.int32), axis=1)
    level = (node >= 4).astype(jnp.int32) + (node >= 6).astype(jnp.int32)
    nodes = jnp.arange(7, dtype=jnp.int32)
    grand = parent[parent]
    ancestor = ((nodes[None, :] == parent[:, None]) | (nodes[None, :] == grand[:, None])) & (
        nodes[None, :] != nodes[:, None]
    )
    node_hot = (node[:, None] == nodes[None, :]).astype(jnp.float32)
    perm_hot = (logical[:, None] == ar[None, :]).astype(jnp.float32)
    listed_store = jnp.dot(
        structure.astype(jnp.float32), perm_hot.T, precision=lax.Precision.HIGHEST
    )
    anc_pairs = jnp.dot(
        node_hot,
        jnp.dot(ancestor.astype(jnp.float32), node_hot.T, precision=lax.Precision.HIGHEST),
        precision=lax.Precision.HIGHEST,
    )
    list_pairs = jnp.dot(node_hot, listed_store, precision=lax.Precision.HIGHEST)
    link = (anc_pairs * list_pairs).T > 0.5
    same = node[:, None] == node[None, :]
    return (level, same, link)


def masked(block_rows, mask):
    rblocks, width = mask.shape
    bsz = block_rows.shape[0] // rblocks
    shaped = block_rows.reshape(rblocks, bsz, width, bsz) * mask[:, None, :, None].astype(
        jnp.float32
    )
    return shaped.reshape(block_rows.shape)


def body(factor, rhs, parent, bounds, slot, structure):
    level, same, link = block_masks(parent, bounds, slot, structure)
    first = lax.axis_index("row") * RB
    level_mine = lax.dynamic_slice_in_dim(level, first, RB, 0)
    same_mine = lax.dynamic_slice_in_dim(same, first, RB, 0)
    link_mine = lax.dynamic_slice_in_dim(link, first, RB, 0)
    full_rows = lax.all_gather(factor, "col", axis=1, tiled=True)
    diag_part = masked(full_rows, same_mine)
    link_part = masked(full_rows, link_mine)

    def product(matrix, vector):
        return jnp.dot(
            matrix,
            lax.all_gather(vector, "row", axis=0, tiled=True),
            precision=lax.Precision.HIGHEST,
            preferred_element_type=jnp.float32,
        )

    pieces = [rhs]
    accums = [jnp.zeros(p.shape, jnp.float32) for p in pieces]
    results = [jnp.zeros(p.shape, jnp.float32) for p in pieces]
    for section in range(3):
        rows = jnp.repeat(level_mine == section, B)[:, None]
        solved = jnp.where(rows, product(diag_part, pieces[0] - accums[0]), 0.0)
        results[0] = results[0] + solved
        if section < 2:
            accums[0] = accums[0] + product(link_part, solved)
    return results[0]


def solution(mesh):
    in_specs = (P("row", "col"), P("row", "col"), P(), P(), P(), P())
    out_specs = P("row", "col")
    return jax.shard_map(body, mesh=mesh, in_specs=in_specs, out_specs=out_specs, check_vma=False)
```

profile of v0, /device:TPU:1, one launch (start us, length us, event | category | flops | bytes accessed | tf_op | source)
XLA Modules:
  0.0 501.4 jit_solution(158808282834339269)
XLA Ops:
  6.5 0.7 all-gather.7.cloned.1.call-update
  7.3 0.7 all-gather.9.cloned.1.call-update
  8.1 0.7 slice.3
  8.8 0.7 select_reduce_fusion
  9.6 0.6 dynamic-slice
  10.2 0.7 dynamic_slice.9
  11.6 0.7 fusion.48
  12.3 51.4 %all-gather.7.cloned.1.call-done = f32[128,8192]{1,0:T(8,128)} async-done(((f32[128,2048]{1,0:T(8,128)}), f32[128,8192]{1,0:T(8,128)}) %all-gather.7.cloned.1.call-update) | async-done | bytes 4194320 | tf_op jit(solution)/shard_map/all_gather | solution.py:52
  63.8 82.7 %all-gather.9.cloned.1.call-done = f32[8192,128]{1,0:T(8,128)} async-done(((f32[128,128]{1,0:T(8,128)}), f32[8192,128]{1,0:T(8,128)}) %all-gather.9.cloned.1.call-update) | async-done | bytes 4194320 | tf_op jit(solution)/shard_map/all_gather | solution.py:59
  146.5 8.4 %fusion.15 = f32[128,128]{1,0:T(8,128)} fusion(f32[8192,128]{1,0:T(8,128)} %all-gather.9.cloned.1.call-done, f32[128,8192]{1,0:T(8,128)} %all-gather.7.cloned.1.call-done, f32[8192]{0:T(1024)S(1)} %broadcast_bitcast_fusion.1, pred[]{:T(512)} %bitcast), kind=kOutput, calls=%fused_computation.16 | convolution fusion | flops 1611677696 | bytes 8486913 | tf_op jit(solution)/shard_map/dot_general | solution.py:57
  155.0 0.6 gather_fusion
  155.6 0.2 fusion.35
  155.8 0.2 fusion.36
  156.0 0.3 fusion.33
  156.3 0.2 fusion.34
  156.7 74.7 %all-gather.11.cloned.1.call-done = f32[8192,128]{1,0:T(8,128)} async-done(((f32[128,128]{1,0:T(8,128)}), f32[8192,128]{1,0:T(8,128)}) %all-gather.11.cloned.1.call-update) | async-done | bytes 4194320 | tf_op jit(solution)/shard_map/all_gather | solution.py:59
  231.4 8.4 %fusion.50 = (f32[128,128]{1,0:T(8,128)}, f32[128,128]{1,0:T(8,128)S(1)}) fusion(f32[128,128]{1,0:T(8,128)S(1)} %copy-done.1, f32[8192,128]{1,0:T(8,128)} %all-gather.11.cloned.1.call-done, f32[128,8192]{1,0:T(8,128)} %all-gather.7.cloned.1.call-done, f32[8192]{0:T(1024)S(1)} %broadcast_bitcast_fusion), kind=kOutput, calls=%fused_computation.55 | convolution fusion | flops 1611677696 | bytes 8617984 | tf_op jit(solution)/shard_map/dot_general | solution.py:57
  239.8 0.2 all-gather.15.cloned.1.call-start
  240.7 75.6 %all-gather.13.cloned.1.call-done = f32[8192,128]{1,0:T(8,128)} async-done(((f32[128,128]{1,0:T(8,128)}), f32[8192,128]{1,0:T(8,128)}) %all-gather.13.cloned.1.call-update) | async-done | bytes 4194320 | tf_op jit(solution)/shard_map/all_gather | solution.py:59
  316.3 8.4 %fusion.18 = f32[128,128]{1,0:T(8,128)} fusion(f32[8192,128]{1,0:T(8,128)} %all-gather.13.cloned.1.call-done, f32[128,8192]{1,0:T(8,128)} %all-gather.7.cloned.1.call-done, f32[8192]{0:T(1024)S(1)} %broadcast_bitcast_fusion.1, pred[]{:T(512)} %bitcast.3), kind=kOutput, calls=%fused_computation.17 | convolution fusion | flops 1611677696 | bytes 8486913 | tf_op jit(solution)/shard_map/dot_general | solution.py:57
  324.8 76.4 %all-gather.15.cloned.1.call-done = f32[8192,128]{1,0:T(8,128)} async-done(((f32[128,128]{1,0:T(8,128)}), f32[8192,128]{1,0:T(8,128)}) %all-gather.15.cloned.1.call-update) | async-done | bytes 4194320 | tf_op jit(solution)/shard_map/all_gather | solution.py:59
  401.2 8.4 %fusion.30 = f32[128,128]{1,0:T(8,128)} fusion(f32[128,128]{1,0:T(8,128)S(1)} %copy-done.1, f32[128,128]{1,0:T(8,128)S(1)} %get-tuple-element.6, f32[8192,128]{1,0:T(8,128)} %all-gather.15.cloned.1.call-done, f32[128,8192]{1,0:T(8,128)} %all-gather.7.cloned.1.call-done, f32[8192]{0:T(1024)S(1)} %broadcast_bitcast_fusion), kind=kOutput, calls=%fused_computation.21 | convolution fusion | flops 1611694080 | bytes 8617984 | tf_op jit(solution)/shard_map/dot_general | solution.py:57
  410.3 75.8 %all-gather.17.cloned.1.call-done = f32[8192,128]{1,0:T(8,128)} async-done(((f32[128,128]{1,0:T(8,128)}), f32[8192,128]{1,0:T(8,128)}) %all-gather.17.cloned.1.call-update) | async-done | bytes 4194320 | tf_op jit(solution)/shard_map/all_gather | solution.py:59
  486.1 8.4 %fusion.24 = f32[128,128]{1,0:T(8,128)} fusion(f32[8192,128]{1,0:T(8,128)} %all-gather.17.cloned.1.call-done, f32[128,8192]{1,0:T(8,128)} %all-gather.7.cloned.1.call-done, f32[8192]{0:T(1024)S(1)} %broadcast_bitcast_fusion.1, f32[128,128]{1,0:T(8,128)S(1)} %copy-done.2, f32[128,128]{1,0:T(8,128)S(1)} %copy-done.3, pred[]{:T(512)} %bitcast.6), kind=kOutput, calls=%fused_computation.19 | convolution fusion | flops 1611710464 | bytes 8617985 | tf_op jit(solution)/shard_map/dot_general | solution.py:57
  (26 shorter events, 0.5 us)
Async XLA Ops:
  6.5 57.2 %all-gather.7.cloned.1.call-start = ((), (), s32[]{:S(2)}) async-start(), calls=%async_computation | async-start | bytes 5242880 | tf_op jit(solution)/shard_map/all_gather | solution.py:52
  7.3 139.2 %all-gather.9.cloned.1.call-start = ((), (), s32[]{:S(2)}) async-start(), calls=%async_computation.1 | async-start | bytes 4259840 | tf_op jit(solution)/shard_map/all_gather | solution.py:59
  8.0 223.4 %all-gather.11.cloned.1.call-start = ((), (), s32[]{:S(2)}) async-start(), calls=%async_computation.2 | async-start | bytes 4259840 | tf_op jit(solution)/shard_map/all_gather | solution.py:59
  146.5 8.5 %copy-start = (s32[7]{0:T(128)S(1)}, s32[7]{0:T(128)}, u32[]{:S(2)}) copy-start(s32[7]{0:T(128)} %param.8) | copy-start | bytes 88
  146.5 9.4 %copy-start.4 = (s32[7,64]{1,0:T(8,128)S(1)}, s32[7,64]{1,0:T(8,128)}, u32[]{:S(2)}) copy-start(s32[7,64]{1,0:T(8,128)} %param.11) | copy-start | bytes 5380
  146.5 84.9 %copy-start.1 = (f32[128,128]{1,0:T(8,128)S(1)}, f32[128,128]{1,0:T(8,128)}, u32[]{:S(2)}) copy-start(f32[128,128]{1,0:T(8,128)} %param.7) | copy-start | bytes 196612
  154.9 161.4 %all-gather.13.cloned.1.call-start = ((), (), s32[]{:S(2)}) async-start(), calls=%async_computation.3 | async-start | bytes 4259840 | tf_op jit(solution)/shard_map/all_gather | solution.py:59
  239.8 161.4 %all-gather.15.cloned.1.call-start = ((), (), s32[]{:S(2)}) async-start(), calls=%async_computation.4 | async-start | bytes 4259840 | tf_op jit(solution)/shard_map/all_gather | solution.py:59
  324.7 161.4 %all-gather.17.cloned.1.call-start = ((), (), s32[]{:S(2)}) async-start(), calls=%async_computation.5 | async-start | bytes 4259840 | tf_op jit(solution)/shard_map/all_gather | solution.py:59
  401.2 84.9 %copy-start.2 = (f32[128,128]{1,0:T(8,128)S(1)}, f32[128,128]{1,0:T(8,128)}, u32[]{:S(2)}) copy-start(f32[128,128]{1,0:T(8,128)} %fusion.15) | copy-start | bytes 196612
  401.2 84.9 %copy-start.3 = (f32[128,128]{1,0:T(8,128)S(1)}, f32[128,128]{1,0:T(8,128)}, u32[]{:S(2)}) copy-start(f32[128,128]{1,0:T(8,128)} %fusion.18) | copy-start | bytes 196612
Sparse Core Ops, SparseCore 0:
  9.2 54.5 all-gather.6
  66.5 79.8 all-gather.8
  155.0 76.3 all-gather.10
  239.9 76.3 all-gather.12
  324.8 76.3 all-gather.14
  409.8 76.3 all-gather.16
where the time goes:
time: 501 us
  waiting for transfers between devices  438 us (87%)
  matrix products  42.9 us (9%)
  between operations  15.6 us (3%)
    all_gather x5, waiting for transfers between devices, product(): lax.all_gather(vector, 'row', axis=0, tiled=True)  385 us
    all_gather x1, waiting for transfers between devices, body(): full_rows = lax.all_gather(factor, 'col', axis=1, tiled=True)  51.4 us
    dot_general x5, matrix products, product(): jnp.dot(matrix, lax.all_gather(vector, 'row', axis=0, tiled=True), precis...  42 us
  transfers between devices with their start and end apart: 6, of which 6 were waited for; matrix products, arithmetic and copies ran while one was open for 1% of the time, Pallas kernels for 0%

commit v1 on v0

--- a/solution.py
+++ b/solution.py
@@ -49,7 +49,14 @@
     level_mine = lax.dynamic_slice_in_dim(level, first, RB, 0)
     same_mine = lax.dynamic_slice_in_dim(same, first, RB, 0)
     link_mine = lax.dynamic_slice_in_dim(link, first, RB, 0)
-    full_rows = lax.all_gather(factor, "col", axis=1, tiled=True)
+    size = lax.axis_size("col")
+    right = [(i, (i + 1) % size) for i in range(size)]
+    parts = [factor]
+    for far in range(1, size):
+        parts = [lax.ppermute(parts[0], "col", right), *parts]
+    out = jnp.concatenate(parts, axis=1)
+    offset = (lax.axis_index("col") + 1) * parts[-1].shape[1]
+    full_rows = jnp.roll(out, offset, axis=1)
     diag_part = masked(full_rows, same_mine)
     link_part = masked(full_rows, link_mine)
 

time: 501 us -> 453 us (0.904)
  waiting for transfers between devices: 438 us -> 375 us
  local copies, waits for them, and re-layouts: 2.79 us -> 13.5 us
  starting transfers between devices: 0.38 us -> 5.41 us
    all_gather x5, waiting for transfers between devices: 385 us -> 313 us  [product(): lax.all_gather(vector, 'row', axis=0, tiled=True)]
    ppermute x0 -> x3, waiting for transfers between devices: none -> 61.4 us  [body(): parts = [lax.ppermute(parts[0], 'col', right), *parts]]
    all_gather x1 -> x0, waiting for transfers between devices: 51.4 us -> none  [body(): full_rows = lax.all_gather(factor, 'col', axis=1, tiled=True)]
    unnamed x10 -> x19, local copies, waits for them, and re-layouts: 0.02 us -> 9.8 us
  transfers between devices with their start and end apart: 6 -> 8, of which waited for: 6 -> 8; matrix products, arithmetic and copies ran while one was open for 1% -> 4% of each run, Pallas kernels for 0% -> 0%
where the time goes in v1:
time: 453 us
  waiting for transfers between devices  375 us (83%)
  matrix products  42.9 us (9%)
  between operations  15.1 us (3%)
  local copies, waits for them, and re-layouts  13.5 us (3%)
  starting transfers between devices  5.41 us (1%)
    all_gather x5, waiting for transfers between devices, product(): lax.all_gather(vector, 'row', axis=0, tiled=True)  313 us
    ppermute x3, waiting for transfers between devices, body(): parts = [lax.ppermute(parts[0], 'col', right), *parts]  61.4 us
    dot_general x5, matrix products, product(): jnp.dot(matrix, lax.all_gather(vector, 'row', axis=0, tiled=True), precis...  42 us
    unnamed x19, local copies, waits for them, and re-layouts  9.8 us
  transfers between devices with their start and end apart: 8, of which 8 were waited for; matrix products, arithmetic and copies ran while one was open for 4% of the time, Pallas kernels for 0%

profile of v1, /device:TPU:1, one launch (start us, length us, event | category | flops | bytes accessed | tf_op | source)
XLA Modules:
  0.0 453.2 jit_solution(13086254248390971808)
XLA Ops:
  7.3 2.1 collective-permute-start
  9.4 22.1 %collective-permute-done = f32[128,2048]{1,0:T(8,128)S(1)} collective-permute-done((f32[128,2048]{1,0:T(8,128)}, f32[128,2048]{1,0:T(8,128)S(1)}, u32[]{:S(2)}, u32[]{:S(2)}) %collective-permute-start) | collective-permute-done | bytes 1048608 | tf_op jit(solution)/shard_map/ppermute | solution.py:56
  31.5 1.9 collective-permute-start.1
  33.4 22.0 %collective-permute-done.1 = f32[128,2048]{1,0:T(8,128)S(1)} collective-permute-done((f32[128,2048]{1,0:T(8,128)S(1)}, f32[128,2048]{1,0:T(8,128)S(1)}, u32[]{:S(2)}, u32[]{:S(2)}) %collective-permute-start.1) | collective-permute-done | bytes 1048608 | tf_op jit(solution)/shard_map/ppermute | solution.py:56
  55.4 0.8 collective-permute-start.2
  60.3 17.3 %collective-permute-done.2 = f32[128,2048]{1,0:T(8,128)} collective-permute-done((f32[128,2048]{1,0:T(8,128)S(1)}, f32[128,2048]{1,0:T(8,128)}, u32[]{:S(2)}, u32[]{:S(2)}) %collective-permute-start.2) | collective-permute-done | bytes 1048608 | tf_op jit(solution)/shard_map/ppermute | solution.py:56
  77.6 2.3 constant_dynamic-update-slice_fusion.7
  80.0 1.0 constant_dynamic-update-slice_fusion.6
  81.0 1.1 constant_dynamic-update-slice_fusion.5
  82.1 1.0 constant_dynamic-update-slice_fusion.4
  83.1 2.3 constant_dynamic-update-slice_fusion.3
  85.4 1.0 constant_dynamic-update-slice_fusion.2
  86.4 1.0 constant_dynamic-update-slice_fusion.1
  87.4 1.0 constant_dynamic-update-slice_fusion
  88.5 5.0 %all-gather.6.cloned.1.call-done = f32[8192,128]{1,0:T(8,128)} async-done(((f32[128,128]{1,0:T(8,128)}), f32[8192,128]{1,0:T(8,128)}) %all-gather.6.cloned.1.call-update) | async-done | bytes 4194320 | tf_op jit(solution)/shard_map/all_gather | solution.py:66
  93.5 8.4 %fusion.20 = f32[128,128]{1,0:T(8,128)} fusion(f32[8192,128]{1,0:T(8,128)} %all-gather.6.cloned.1.call-done, f32[128,16384]{1,0:T(8,128)} %constant_dynamic-update-slice_fusion, s32[]{:T(128)S(6)} %select_n.38, f32[8192]{0:T(1024)S(1)} %broadcast_bitcast_fusion.1, pred[]{:T(512)} %bitcast), kind=kOutput, calls=%fused_computation.21 | convolution fusion | flops 1611677696 | bytes 8487428 | tf_op jit(solution)/shard_map/dot_general | solution.py:64
  103.9 79.8 %all-gather.8.cloned.1.call-done = f32[8192,128]{1,0:T(8,128)} async-done(((f32[128,128]{1,0:T(8,128)}), f32[8192,128]{1,0:T(8,128)}) %all-gather.8.cloned.1.call-update) | async-done | bytes 4194320 | tf_op jit(solution)/shard_map/all_gather | solution.py:66
  183.6 8.4 %fusion.60 = (f32[128,128]{1,0:T(8,128)}, f32[128,128]{1,0:T(8,128)S(1)}) fusion(f32[128,128]{1,0:T(8,128)S(1)} %copy-done.2, f32[8192,128]{1,0:T(8,128)} %all-gather.8.cloned.1.call-done, f32[128,16384]{1,0:T(8,128)} %constant_dynamic-update-slice_fusion, s32[]{:T(128)S(6)} %select_n.38, f32[8192]{0:T(1024)S(1)} %broadcast_bitcast_fusion), kind=kOutput, calls=%fused_computation.75 | convolution fusion | flops 1611677696 | bytes 8617988 | tf_op jit(solution)/shard_map/dot_general | solution.py:64
  192.7 75.8 %all-gather.10.cloned.1.call-done = f32[8192,128]{1,0:T(8,128)} async-done(((f32[128,128]{1,0:T(8,128)}), f32[8192,128]{1,0:T(8,128)}) %all-gather.10.cloned.1.call-update) | async-done | bytes 4194320 | tf_op jit(solution)/shard_map/all_gather | solution.py:66
  268.5 8.4 %fusion.23 = f32[128,128]{1,0:T(8,128)} fusion(f32[8192,128]{1,0:T(8,128)} %all-gather.10.cloned.1.call-done, f32[128,16384]{1,0:T(8,128)} %constant_dynamic-update-slice_fusion, s32[]{:T(128)S(6)} %select_n.38, f32[8192]{0:T(1024)S(1)} %broadcast_bitcast_fusion.1, pred[]{:T(512)} %bitcast.3), kind=kOutput, calls=%fused_computation.22 | convolution fusion | flops 1611677696 | bytes 8487428 | tf_op jit(solution)/shard_map/dot_general | solution.py:64
  277.2 76.2 %all-gather.12.cloned.1.call-done = f32[8192,128]{1,0:T(8,128)} async-done(((f32[128,128]{1,0:T(8,128)}), f32[8192,128]{1,0:T(8,128)}) %all-gather.12.cloned.1.call-update) | async-done | bytes 4194320 | tf_op jit(solution)/shard_map/all_gather | solution.py:66
  353.4 8.4 %fusion.32 = f32[128,128]{1,0:T(8,128)} fusion(f32[128,128]{1,0:T(8,128)S(1)} %copy-done.2, f32[128,128]{1,0:T(8,128)S(1)} %get-tuple-element.6, f32[8192,128]{1,0:T(8,128)} %all-gather.12.cloned.1.call-done, f32[128,16384]{1,0:T(8,128)} %constant_dynamic-update-slice_fusion, s32[]{:T(128)S(6)} %select_n.38, f32[8192]{0:T(1024)S(1)} %broadcast_bitcast_fusion), kind=kOutput, calls=%fused_computation.25 | convolution fusion | flops 1611694080 | bytes 8617988 | tf_op jit(solution)/shard_map/dot_general | solution.py:64
  362.5 75.8 %all-gather.14.cloned.1.call-done = f32[8192,128]{1,0:T(8,128)} async-done(((f32[128,128]{1,0:T(8,128)}), f32[8192,128]{1,0:T(8,128)}) %all-gather.14.cloned.1.call-update) | async-done | bytes 4194320 | tf_op jit(solution)/shard_map/all_gather | solution.py:66
  438.3 8.4 %add_add_fusion = f32[128,128]{1,0:T(8,128)} fusion(f32[128,128]{1,0:T(8,128)S(1)} %copy-done.3, f32[128,128]{1,0:T(8,128)S(1)} %copy-done.4, f32[8192,128]{1,0:T(8,128)} %all-gather.14.cloned.1.call-done, f32[128,16384]{1,0:T(8,128)} %constant_dynamic-update-slice_fusion, s32[]{:T(128)S(6)} %select_n.38, f32[8192]{0:T(1024)S(1)} %broadcast_bitcast_fusion.1, ...), kind=kOutput, calls=%fused_computation.26 | convolution fusion | flops 1611710464 | bytes 8618500 | tf_op jit(solution)/shard_map/dot_general | solution.py:64
  (39 shorter events, 6.5 us)
Async XLA Ops:
  6.5 75.5 %copy-start.1 = (f32[128,2048]{1,0:T(8,128)S(1)}, f32[128,2048]{1,0:T(8,128)}, u32[]{:S(2)}) copy-start(f32[128,2048]{1,0:T(8,128)} %param.6) | copy-start | bytes 3145732
  6.5 87.0 %all-gather.6.cloned.1.call-start = ((), (), s32[]{:S(2)}) async-start(), calls=%async_computation | async-start | bytes 4259840 | tf_op jit(solution)/shard_map/all_gather | solution.py:66
  7.3 176.4 %all-gather.8.cloned.1.call-start = ((), (), s32[]{:S(2)}) async-start(), calls=%async_computation.1 | async-start | bytes 4259840 | tf_op jit(solution)/shard_map/all_gather | solution.py:66
  7.3 24.2 %collective-permute-start = (f32[128,2048]{1,0:T(8,128)}, f32[128,2048]{1,0:T(8,128)S(1)}, u32[]{:S(2)}, u32[]{:S(2)}) collective-permute-start(f32[128,2048]{1,0:T(8,128)} %param.6), channel_id=1, source_target_pairs={{0,1},{1,2},{2,3},{3,0},{4,5},{5,6},{6,7},{7,4},{8,9},{9,10},{10,1... | collective-permute-start | bytes 3145736 | tf_op jit(solution)/shard_map/ppermute | solution.py:56
  31.5 23.9 %collective-permute-start.1 = (f32[128,2048]{1,0:T(8,128)S(1)}, f32[128,2048]{1,0:T(8,128)S(1)}, u32[]{:S(2)}, u32[]{:S(2)}) collective-permute-start(f32[128,2048]{1,0:T(8,128)S(1)} %collective-permute-done), channel_id=1, source_target_pairs={{0,1},{1,2},{2,3},{3,0},{4,5},{5,6},{6,7},{7,4},{8,9},{9,10},{10,1... | collective-permute-start | bytes 3145736 | tf_op jit(solution)/shard_map/ppermute | solution.py:56
  55.4 22.3 %collective-permute-start.2 = (f32[128,2048]{1,0:T(8,128)S(1)}, f32[128,2048]{1,0:T(8,128)}, u32[]{:S(2)}, u32[]{:S(2)}) collective-permute-start(f32[128,2048]{1,0:T(8,128)S(1)} %collective-permute-done.1), channel_id=1, source_target_pairs={{0,1},{1,2},{2,3},{3,0},{4,5},{5,6},{6,7},{7,4},{8,9},{9,10},{10,1... | collective-permute-start | bytes 3145736 | tf_op jit(solution)/shard_map/ppermute | solution.py:56
  93.5 8.7 %copy-start = (s32[7]{0:T(128)S(1)}, s32[7]{0:T(128)}, u32[]{:S(2)}) copy-start(s32[7]{0:T(128)} %param.8) | copy-start | bytes 88
  93.5 9.6 %copy-start.5 = (s32[7,64]{1,0:T(8,128)S(1)}, s32[7,64]{1,0:T(8,128)}, u32[]{:S(2)}) copy-start(s32[7,64]{1,0:T(8,128)} %param.11) | copy-start | bytes 5380
  93.5 90.1 %copy-start.2 = (f32[128,128]{1,0:T(8,128)S(1)}, f32[128,128]{1,0:T(8,128)}, u32[]{:S(2)}) copy-start(f32[128,128]{1,0:T(8,128)} %param.7) | copy-start | bytes 196612
  101.9 166.6 %all-gather.10.cloned.1.call-start = ((), (), s32[]{:S(2)}) async-start(), calls=%async_computation.2 | async-start | bytes 4259840 | tf_op jit(solution)/shard_map/all_gather | solution.py:66
  192.0 161.4 %all-gather.12.cloned.1.call-start = ((), (), s32[]{:S(2)}) async-start(), calls=%async_computation.3 | async-start | bytes 4259840 | tf_op jit(solution)/shard_map/all_gather | solution.py:66
  276.9 161.4 %all-gather.14.cloned.1.call-start = ((), (), s32[]{:S(2)}) async-start(), calls=%async_computation.4 | async-start | bytes 4259840 | tf_op jit(solution)/shard_map/all_gather | solution.py:66
  353.4 84.9 %copy-start.3 = (f32[128,128]{1,0:T(8,128)S(1)}, f32[128,128]{1,0:T(8,128)}, u32[]{:S(2)}) copy-start(f32[128,128]{1,0:T(8,128)} %fusion.20) | copy-start | bytes 196612
  353.4 84.9 %copy-start.4 = (f32[128,128]{1,0:T(8,128)S(1)}, f32[128,128]{1,0:T(8,128)}, u32[]{:S(2)}) copy-start(f32[128,128]{1,0:T(8,128)} %fusion.23) | copy-start | bytes 196612
Sparse Core Ops, SparseCore 0:
  10.1 83.3 all-gather.5
  102.1 81.5 all-gather.7
  192.2 76.3 all-gather.9
  277.0 76.3 all-gather.11
  362.0 76.3 all-gather.13
